TPU v7x, 256 devices: a whole 4x4x8 slice. The times are simulated.
256 devices in a mesh: inner: 16 (over x, y), outer: 16 (over z, core).
Axes of the slice: x: 4, y: 4, z: 8, core: 2. Of those that a mesh axis runs over, the one named last changes fastest.
Arguments:
- tokens: int32 [4096], P('outer'), may hold values from 0 to 16383
- step_index: int32 [1], replicated, may hold values from 0 to 31
- embed_table: bfloat16 [16384, 2048], P(None, 'inner'), may hold values from -6 to 6
- gain_one: float32 [2048], replicated, may hold values from 0.5 to 1.5
- gate_weight: bfloat16 [2048, 5632], P(None, 'inner'), may hold values from -0.125 to 0.125
- up_weight: bfloat16 [2048, 5632], P(None, 'inner'), may hold values from -0.125 to 0.125
- down_weight: bfloat16 [5632, 2048], P('inner'), may hold values from -0.078125 to 0.078125
- gain_two: float32 [2048], replicated, may hold values from 0.5 to 1.5
- query_weight: bfloat16 [2048, 2048], P(None, 'inner'), may hold values from -0.125 to 0.125
- key_weight: bfloat16 [2048, 2048], P(None, 'inner'), may hold values from -0.125 to 0.125
- value_weight: bfloat16 [2048, 4096], P(None, 'inner'), may hold values from -0.125 to 0.125
- decay_weight: bfloat16 [2048, 16], P(None, 'inner'), may hold values from -0.125 to 0.125
- beta_weight: bfloat16 [2048, 16], P(None, 'inner'), may hold values from -0.125 to 0.125
- rate_log: float32 [16], P('inner'), may hold values from -12 to -2
- decay_bias: float32 [16], P('inner'), may hold values from -1 to 1
- beta_bias: float32 [16], P('inner'), may hold values from -6 to -2
- cotangent: bfloat16 [4096, 4096], P('outer', 'inner'), may hold values from -192 to 192
Outputs:
- attribution: float32 [4096, 5632], P('outer', 'inner')
All inputs are finite; a program needn't handle non-finite values.
Results may differ from a plain program's by a relative error of at most 0.029.
Values may be sent and summed in bfloat16 or wider, within the bound.
A program may use at most 128 MiB of HBM per device.

v0:
```python
import functools
import math
import jax
import jax.numpy as jnp
from jax import lax
from jax.sharding import PartitionSpec as P

STEPS = 32


def from_behind(array, axis, by):
    devices = lax.axis_size(axis)
    pairs = [(i, i + by) for i in range(devices) if 0 <= i + by < devices]
    return lax.ppermute(array, axis, pairs)


def unit_rows(values):
    return values * lax.rsqrt(jnp.sum(values * values, axis=-1, keepdims=True) + 1e-06)


def head_inputs(query_rows, key_rows, decay_rows, beta_rows, log_rate, rate_shift, beta_shift):
    queries = unit_rows(query_rows) * query_rows.shape[-1] ** (-0.5)
    keys_unit = unit_rows(key_rows)
    log_decay = -jnp.exp(log_rate) * jax.nn.softplus(decay_rows + rate_shift)
    betas = jax.nn.sigmoid(beta_rows + beta_shift)
    return (queries, keys_unit, log_decay, betas)


def block_step(with_out, state, pieces):
    queries, keys_unit, values, log_decay, betas = pieces
    block_len = keys_unit.shape[0]
    highest = lax.Precision.HIGHEST
    cum_decay = jnp.cumsum(log_decay)
    row_ids = jnp.arange(block_len)[:, None]
    col_ids = jnp.arange(block_len)[None, :]
    lower_mask = row_ids >= col_ids
    decay_mat = jnp.where(
        lower_mask,
        jnp.exp(jnp.where(lower_mask, cum_decay[:, None] - cum_decay[None, :], 0.0)),
        0.0,
    )
    key_gram = jnp.dot(keys_unit, keys_unit.T, precision=highest)
    strict = jnp.where(row_ids > col_ids, betas[:, None] * decay_mat * key_gram, 0.0)
    system = strict + jnp.eye(block_len, dtype=jnp.float32)
    start_scale = jnp.exp(cum_decay)[:, None]
    target = betas[:, None] * (values - start_scale * jnp.dot(keys_unit, state, precision=highest))
    fresh_vals = lax.linalg.triangular_solve(
        system, target, left_side=True, lower=True, unit_diagonal=True
    )
    tail_keys = jnp.exp(cum_decay[-1] - cum_decay)[:, None] * keys_unit
    new_state = jnp.exp(cum_decay[-1]) * state + jnp.dot(tail_keys.T, fresh_vals, precision=highest)
    if with_out:
        scores = decay_mat * jnp.dot(queries, keys_unit.T, precision=highest)
        output = start_scale * jnp.dot(queries, state, precision=highest) + jnp.dot(
            scores, fresh_vals, precision=highest
        )
        return (new_state, output)
    return (new_state, None)


def run_blocks(queries, keys_unit, values, log_decay, betas, state, with_out):
    length = keys_unit.shape[0]
    block_len = math.gcd(64, length)
    block_count = length // block_len

    def blocked(array):
        return array.reshape((block_count, block_len) + array.shape[1:])

    step_fn = functools.partial(block_step, with_out)
    final_state, outputs = lax.scan(
        step_fn,
        state,
        (blocked(queries), blocked(keys_unit), blocked(values), blocked(log_decay), blocked(betas)),
    )
    if with_out:
        outputs = outputs.reshape((length,) + outputs.shape[2:])
    return (final_state, outputs)


def rms_scaled(values, gain):
    return values * lax.rsqrt(jnp.mean(values * values, axis=-1, keepdims=True) + 1e-06) * gain


def apply_map(matrix, state):
    return jnp.einsum("hij,hjv->hiv", matrix, state, precision=lax.Precision.HIGHEST)


def shards(
    tokens,
    step_index,
    embed_table,
    gain_one,
    gate_weight,
    up_weight,
    down_weight,
    gain_two,
    query_weight,
    key_weight,
    value_weight,
    decay_weight,
    beta_weight,
    rate_log,
    decay_bias,
    beta_bias,
    cotangent,
):
    columns = jnp.take(embed_table, tokens, axis=0)
    embedded = lax.all_gather(columns, "inner", axis=1, tiled=True)
    emb_float = embedded.astype(jnp.float32)
    normed_one = rms_scaled(emb_float, gain_one).astype(jnp.bfloat16)
    gate_rows = jnp.dot(normed_one, gate_weight, preferred_element_type=jnp.float32)
    up_rows = jnp.dot(normed_one, up_weight, preferred_element_type=jnp.float32)
    hidden = jax.nn.silu(gate_rows) * up_rows
    path_scale = (step_index[0].astype(jnp.float32) + 0.5) / STEPS
    scaled = (path_scale * hidden).astype(jnp.bfloat16)
    group_rows = tokens.shape[0]
    row_share = group_rows // lax.axis_size("inner")
    head_count = rate_log.shape[0]
    key_dim = query_weight.shape[1] // head_count
    value_dim = value_weight.shape[1] // head_count
    main_weight = jnp.concatenate([query_weight, key_weight, value_weight], axis=1)
    gate_pair = jnp.concatenate([decay_weight, beta_weight], axis=1)

    def normalize(values):
        return rms_scaled(values, gain_two)

    mixed_share = lax.psum_scatter(
        jnp.dot(scaled, down_weight, preferred_element_type=jnp.float32).astype(jnp.bfloat16),
        "inner",
        scatter_dimension=0,
        tiled=True,
    ).astype(jnp.float32)
    own_rows = lax.dynamic_slice_in_dim(
        emb_float, lax.axis_index("inner") * row_share, row_share, 0
    )
    normed_float, norm_pull = jax.vjp(normalize, own_rows + mixed_share)
    block_piece = lax.all_gather(normed_float.astype(jnp.bfloat16), "inner", axis=0, tiled=True)
    main_part = jnp.dot(block_piece, main_weight, preferred_element_type=jnp.float32)
    gate_part = jnp.dot(block_piece, gate_pair, preferred_element_type=jnp.float32)
    projected = jnp.concatenate([main_part, gate_part], axis=1)
    key_span = head_count * key_dim
    value_span = head_count * value_dim

    def by_head(columns_block, width):
        return columns_block.reshape(group_rows, head_count, width).transpose(1, 0, 2)

    query_pre = by_head(projected[:, :key_span], key_dim)
    key_pre = by_head(projected[:, key_span : 2 * key_span], key_dim)
    value_pre = by_head(projected[:, 2 * key_span : 2 * key_span + value_span], value_dim)
    gate_start = 2 * key_span + value_span
    decay_pre = projected[:, gate_start : gate_start + head_count].T
    beta_pre = projected[:, gate_start + head_count : gate_start + 2 * head_count].T
    cot_heads = by_head(cotangent.astype(jnp.float32), value_dim)

    def carry_map(key_rows, value_rows, decay_rows, beta_rows, log_rate, rate_shift, beta_shift):
        unused_query, keys_unit, log_decay, betas = head_inputs(
            key_rows, key_rows, decay_rows, beta_rows, log_rate, rate_shift, beta_shift
        )
        padded_vals = jnp.concatenate(
            [value_rows, jnp.zeros((key_rows.shape[0], key_dim), jnp.float32)], axis=1
        )
        start_state = jnp.concatenate(
            [jnp.zeros((key_dim, value_dim), jnp.float32), jnp.eye(key_dim, dtype=jnp.float32)],
            axis=1,
        )
        final_state, unused_out = run_blocks(
            keys_unit, keys_unit, padded_vals, log_decay, betas, start_state, False
        )
        return final_state

    joined_state = jax.vmap(carry_map)(
        key_pre, value_pre, decay_pre, beta_pre, rate_log, decay_bias, beta_bias
    )
    offset_state = joined_state[:, :, :value_dim]
    transition = joined_state[:, :, value_dim:]

    def forward_step(turn_index, carried):
        incoming = from_behind(carried[1].astype(jnp.bfloat16), "outer", 1).astype(jnp.float32)
        return (incoming, apply_map(transition, incoming) + offset_state)

    state_in, unused_end = lax.fori_loop(
        0, lax.axis_size("outer") - 1, forward_step, (jnp.zeros_like(offset_state), offset_state)
    )

    def local_score(query_in, key_in, value_in, decay_in, beta_in, start_in):

        def one_head(
            query_rows,
            key_rows,
            value_rows,
            decay_rows,
            beta_rows,
            start_state,
            cot_rows,
            log_rate,
            rate_shift,
            beta_shift,
        ):
            queries, keys_unit, log_decay, betas = head_inputs(
                query_rows, key_rows, decay_rows, beta_rows, log_rate, rate_shift, beta_shift
            )
            final_state, outputs = run_blocks(
                queries, keys_unit, value_rows, log_decay, betas, start_state, True
            )
            return (jnp.sum(outputs * cot_rows), final_state)

        head_scores, final_states = jax.vmap(one_head)(
            query_in,
            key_in,
            value_in,
            decay_in,
            beta_in,
            start_in,
            cot_heads,
            rate_log,
            decay_bias,
            beta_bias,
        )
        return (jnp.sum(head_scores), final_states)

    score_pair, pull_back = jax.vjp(
        local_score, query_pre, key_pre, value_pre, decay_pre, beta_pre, state_in
    )
    first_pull = pull_back((jnp.ones_like(score_pair[0]), jnp.zeros_like(score_pair[1])))
    grad_local = first_pull[5]
    grad_trans = jnp.swapaxes(transition, 1, 2)

    def backward_step(turn_index, carried):
        incoming = from_behind(carried[1].astype(jnp.bfloat16), "outer", -1).astype(jnp.float32)
        return (incoming, apply_map(grad_trans, incoming) + grad_local)

    state_grad, unused_start = lax.fori_loop(
        0, lax.axis_size("outer") - 1, backward_step, (jnp.zeros_like(grad_local), grad_local)
    )
    second_pull = pull_back((jnp.zeros_like(score_pair[0]), state_grad))
    summed = [first_pull[which] + second_pull[which] for which in range(5)]

    def by_rows(head_block):
        return head_block.transpose(1, 0, 2).reshape(group_rows, -1).astype(jnp.bfloat16)

    grad_main = jnp.concatenate(
        [by_rows(summed[0]), by_rows(summed[1]), by_rows(summed[2])], axis=1
    )
    grad_gates = jnp.concatenate(
        [summed[3].T.astype(jnp.bfloat16), summed[4].T.astype(jnp.bfloat16)], axis=1
    )
    main_part = jnp.dot(grad_main, main_weight.T, preferred_element_type=jnp.float32)
    back_share = lax.psum_scatter(
        (main_part + jnp.dot(grad_gates, gate_pair.T, preferred_element_type=jnp.float32)).astype(
            jnp.bfloat16
        ),
        "inner",
        scatter_dimension=0,
        tiled=True,
    ).astype(jnp.float32)
    grad_mixed = norm_pull(back_share)[0].astype(jnp.bfloat16)
    return hidden * jnp.dot(
        lax.all_gather(grad_mixed, "inner", axis=0, tiled=True),
        down_weight.T,
        preferred_element_type=jnp.float32,
    )


def solution(mesh):
    placed = (
        P("outer"),
        P(),
        P(None, "inner"),
        P(),
        P(None, "inner"),
        P(None, "inner"),
        P("inner", None),
        P(),
        P(None, "inner"),
        P(None, "inner"),
        P(None, "inner"),
        P(None, "inner"),
        P(None, "inner"),
        P("inner"),
        P("inner"),
        P("inner"),
        P("outer", "inner"),
    )
    return jax.shard_map(
        shards, mesh=mesh, in_specs=placed, out_specs=P("outer", "inner"), check_vma=False
    )
```

profile of v0, /device:TPU:32, one launch (start us, length us, event | category | flops | bytes accessed | tf_op | source)
XLA Modules:
  0.0 940.6 jit_solution(13554615384378259436)
XLA Ops:
  12.9 50.4 %all-gather.4.cloned.1.call-done = bf16[256,2048]{1,0:T(8,128)(2,1)} async-done(((bf16[256,128]{1,0:T(8,128)(2,1)}), bf16[256,2048]{1,0:T(8,128)(2,1)}) %all-gather.4.cloned.1.call-update) | async-done | bytes 1048592 | tf_op jit(solution)/shard_map/all_gather | solution.py:108
  71.5 75.9 %reduce-scatter.3.cloned.1.call-done = bf16[16,2048]{1,0:T(8,128)(2,1)} async-done(((bf16[256,2048]{1,0:T(8,128)(2,1)}), bf16[16,2048]{1,0:T(8,128)(2,1)}) %reduce-scatter.3.cloned.1.call-update) | async-done | bytes 65552 | tf_op jit(solution)/shard_map/reduce_scatter | solution.py:127
  159.2 38.3 %all-gather.6.cloned.1.call-done = bf16[256,2048]{1,0:T(8,128)(2,1)} async-done(((bf16[16,2048]{1,0:T(8,128)(2,1)}), bf16[256,2048]{1,0:T(8,128)(2,1)}) %all-gather.6.cloned.1.call-update) | async-done | bytes 1048592 | tf_op jit(solution)/shard_map/all_gather | solution.py:137
  207.3 42.3 %while.149 = (s32[]{:T(128)}, f32[1,128,384]{2,1,0:T(8,128)S(1)}, f32[4,1,64]{2,1,0:T(1,128)}, f32[4,1,64,128]{3,2,1,0:T(8,128)S(1)}, f32[4,1,64]{2,1,0:T(1,128)...) while((s32[]{:T(128)}, f32[1,128,384]{2,1,0:T(8,128)S(1)}, f32[4,1,64]{2,1,0:T(1,128)}, ...), condition=%wide.region_6.7_spmd, body=%wide.region_4.6_spmd.sunk | while | flops 100913216 | bytes 1219713 | solution.py:70
  252.6 98.7 %while.150 = (s32[]{:T(128)}, f32[1,128,256]{2,1,0:T(8,128)}, bf16[1,128,256]{2,1,0:T(8,128)(2,1)S(1)}, f32[1,128,128]{2,1,0:T(8,128)S(1)}, f32[1,128,256]{2,1,0:T(8,128)S(1)}, /*index=5*/s32[]{:T(128)}) while((s32[]{:T(128)}, f32[1,128,256]{2,1,0:T(8,128)}, bf16[1,128,256]{2,1,0:T(8,128)(2,1)S(1)}, f32[1,128,128]{2,1,0:T(8,128)S(1)}, ...), condition=%wide.region_8.9_spmd, body=%wide.region_7.8_spmd.sunk | while | flops 50429952 | bytes 786541 | solution.py:181
  336.7 5.1 collective-permute-start
  343.6 5.9 collective-permute-start
  354.1 95.0 %while.152 = (s32[]{:T(128)}, f32[1,128,256]{2,1,0:T(8,128)}, f32[4,1,64,64]{3,2,1,0:T(8,128)}, f32[4,1,128,64]{3,2,1,0:T(8,128)}, f32[4,1,64,64]{3,2,1,0:T(8,12...) while((s32[]{:T(128)}, f32[1,128,256]{2,1,0:T(8,128)}, ...), condition=%wide.region_12.13_spmd.clone.clone, body=%wide.region_10.12_spmd.clone.clone.sunk | while | flops 100962496 | bytes 2558033 | solution.py:70
  451.1 108.1 %while.154 = (s32[]{:T(128)}, f32[1,128,256]{1,2,0:T(8,128)S(1)}, f32[4,1,64,128]{3,2,1,0:T(8,128)}, f32[4,1,64,128]{3,2,1,0:T(8,128)}, f32[4,1,64,256]{3,2,1,0:...) while((s32[]{:T(128)}, f32[1,128,256]{1,2,0:T(8,128)S(1)}, ...), condition=%wide.region_24.27_spmd.clone.clone, body=%wide.region_13.26_spmd.clone.clone.sunk | while | flops 230404480 | bytes 3990816 | solution.py:70
  454.7 4.9 custom-call.51
  481.8 4.9 custom-call.51
  508.8 4.9 custom-call.51
  535.8 4.9 custom-call.51
  560.0 116.6 %while.151 = (s32[]{:T(128)}, f32[1,128,256]{2,1,0:T(8,128)}, bf16[1,128,256]{2,1,0:T(8,128)(2,1)S(1)}, f32[1,128,128]{2,1,0:T(8,128)S(1)}, f32[1,128,256]{2,1,0:T(8,128)S(1)}, /*index=5*/s32[]{:T(128)}) while((s32[]{:T(128)}, f32[1,128,256]{2,1,0:T(8,128)}, bf16[1,128,256]{2,1,0:T(8,128)(2,1)S(1)}, f32[1,128,128]{2,1,0:T(8,128)S(1)}, ...), condition=%wide.region_27.30_spmd, body=%wide.region_26.29_spmd.sunk | while | flops 50429952 | bytes 786541 | solution.py:232
  569.5 5.5 collective-permute-done.1
  585.3 5.5 collective-permute-done.1
  601.2 5.5 collective-permute-done.1
  679.8 102.9 %while.153 = (s32[]{:T(128)}, f32[1,128,256]{1,2,0:T(8,128)S(1)}, f32[4,1,64,128]{3,2,1,0:T(8,128)}, f32[4,1,64,128]{3,2,1,0:T(8,128)}, f32[4,1,64,256]{3,2,1,0:...) while((s32[]{:T(128)}, f32[1,128,256]{1,2,0:T(8,128)S(1)}, ...), condition=%wide.region_39.42_spmd.clone.clone, body=%wide.region_28.41_spmd.clone.clone.sunk | while | flops 230273408 | bytes 4006157 | solution.py:70
  683.4 4.9 custom-call.50
  709.2 4.9 custom-call.50
  734.9 4.9 custom-call.50
  760.6 4.9 custom-call.50
  791.7 89.8 %reduce-scatter.5.cloned.1.call-done = bf16[16,2048]{1,0:T(8,128)(2,1)} async-done(((bf16[256,2048]{1,0:T(8,128)(2,1)}), bf16[16,2048]{1,0:T(8,128)(2,1)}) %reduce-scatter.5.cloned.1.call-update) | async-done | bytes 65552 | tf_op jit(solution)/shard_map/reduce_scatter | solution.py:248
  884.3 47.3 %all-gather.8.cloned.1.call-done = bf16[256,2048]{1,0:T(8,128)(2,1)} async-done(((bf16[16,2048]{1,0:T(8,128)(2,1)}), bf16[256,2048]{1,0:T(8,128)(2,1)}) %all-gather.8.cloned.1.call-update) | async-done | bytes 1048592 | tf_op jit(solution)/shard_map/all_gather | solution.py:258
  (668 shorter events, 538.4 us)
Async XLA Ops:
  6.5 56.8 %all-gather.4.cloned.1.call-start = ((), (), s32[]{:S(2)}) async-start(), calls=%async_computation.2 | async-start | bytes 1114112 | tf_op jit(solution)/shard_map/all_gather | solution.py:108
  12.2 135.2 %reduce-scatter.3.cloned.1.call-start = ((), (), s32[]{:S(2)}) async-start(), calls=%async_computation.3 | async-start | bytes 1114112 | tf_op jit(solution)/shard_map/reduce_scatter | solution.py:127
  69.9 127.6 %all-gather.6.cloned.1.call-start = ((), (), s32[]{:S(2)}) async-start(), calls=%async_computation.4 | async-start | bytes 1114112 | tf_op jit(solution)/shard_map/all_gather | solution.py:137
  150.2 731.3 %reduce-scatter.5.cloned.1.call-start = ((), (), s32[]{:S(2)}) async-start(), calls=%async_computation.5 | async-start | bytes 1114112 | tf_op jit(solution)/shard_map/reduce_scatter | solution.py:248
  259.1 5.6 collective-permute-start
  265.5 5.6 collective-permute-start
  336.7 6.0 collective-permute-start
  343.6 6.8 collective-permute-start
  560.0 6.6 collective-permute-start.1
  567.6 7.4 collective-permute-start.1
  575.9 6.7 collective-permute-start.1
  583.4 7.4 collective-permute-start.1
  591.7 6.6 collective-permute-start.1
  599.3 7.4 collective-permute-start.1
  607.6 6.8 collective-permute-start.1
  615.2 6.8 collective-permute-start.1
  622.9 6.8 collective-permute-start.1
  630.6 6.8 collective-permute-start.1
  638.3 6.8 collective-permute-start.1
  646.0 6.8 collective-permute-start.1
  653.6 6.8 collective-permute-start.1
  661.3 6.8 collective-permute-start.1
  669.0 6.8 collective-permute-start.1
  791.7 139.9 %all-gather.8.cloned.1.call-start = ((), (), s32[]{:S(2)}) async-start(), calls=%async_computation.6 | async-start | bytes 1114112 | tf_op jit(solution)/shard_map/all_gather | solution.py:258
  (52 other events, 2101.4 us)
Sparse Core Ops, SparseCore 0:
  12.4 50.9 all-gather.3
  70.0 77.3 reduce-scatter.2
  150.3 47.1 all-gather.5
  791.8 89.6 reduce-scatter.4
  884.4 47.1 all-gather.7
where the time goes:
time: 948 us; the launch traced here: 941 us
  waiting for transfers between devices  423 us (45%)
  other arithmetic  188 us (20%)
  matrix products  150 us (16%)
  local copies, waits for them, and re-layouts  78.9 us (8%)
  starting transfers between devices  67.8 us (7%)
  loops' own time  17.5 us (2%)
  between operations  16.5 us (2%)
    ppermute x30, waiting for transfers between devices, from_behind(): return lax.ppermute(array, axis, pairs)  121 us
    reduce_scatter x1, waiting for transfers between devices, shards(): lax.psum_scatter((main_part + jnp.dot(grad_gates, gate_pair.T, preferred_...  89.8 us
    another operation x44, other arithmetic, block_step(): lax.linalg.triangular_solve(system, target, left_side=True, lower=True, u...  85.4 us
    reduce_scatter x1, waiting for transfers between devices, shards(): lax.psum_scatter(jnp.dot(scaled, down_weight, preferred_element_type=jnp....  75.9 us
    ppermute x30, starting transfers between devices, from_behind(): return lax.ppermute(array, axis, pairs)  67.6 us
    all_gather x1, waiting for transfers between devices, shards(): embedded = lax.all_gather(columns, 'inner', axis=1, tiled=True)  50.4 us
    all_gather x1, waiting for transfers between devices, shards(): lax.all_gather(grad_mixed, 'inner', axis=0, tiled=True)  47.3 us
    all_gather x1, waiting for transfers between devices, shards(): lax.all_gather(normed_float.astype(jnp.bfloat16), 'inner', axis=0, tiled=...  38.3 us
  transfers between devices with their start and end apart: 35, of which 35 were waited for; matrix products, arithmetic and copies ran while one was open for 1% of the time, Pallas kernels for 0%

commit v1 on v0

--- a/solution.py
+++ b/solution.py
@@ -134,7 +134,17 @@
         emb_float, lax.axis_index("inner") * row_share, row_share, 0
     )
     normed_float, norm_pull = jax.vjp(normalize, own_rows + mixed_share)
-    block_piece = lax.all_gather(normed_float.astype(jnp.bfloat16), "inner", axis=0, tiled=True)
+    x = normed_float.astype(jnp.bfloat16)
+    ways = lax.axis_size("inner")
+    up = [(d, (d + 1) % ways) for d in range(ways)]
+    down = [(d, (d - 1) % ways) for d in range(ways)]
+    earlier, later = ([x], [x])
+    for _ in range(ways // 2):
+        earlier.append(lax.ppermute(earlier[-1], "inner", up))
+    for _ in range((ways - 1) // 2):
+        later.append(lax.ppermute(later[-1], "inner", down))
+    line = jnp.concatenate([*earlier[::-1], *later[1:]], axis=0)
+    block_piece = jnp.roll(line, (lax.axis_index("inner") - ways // 2) * x.shape[0], axis=0)
     main_part = jnp.dot(block_piece, main_weight, preferred_element_type=jnp.float32)
     gate_part = jnp.dot(block_piece, gate_pair, preferred_element_type=jnp.float32)
     projected = jnp.concatenate([main_part, gate_part], axis=1)

time: 948 us -> 977 us (1.031)
  starting transfers between devices: 67.8 us -> 109 us
  waiting for transfers between devices: 423 us -> 404 us
    ppermute x0 -> x15, starting transfers between devices: none -> 40.3 us  [the longest x7 39 us: shards(): later.append(lax.ppermute(later[-1], 'inner', down))]
    all_gather x1 -> x0, waiting for transfers between devices: 38.3 us -> none  [shards(): lax.all_gather(normed_float.astype(jnp.bfloat16), 'inner', axis=0, tiled=...]
    ppermute x0 -> x15, waiting for transfers between devices: none -> 15.9 us  [the longest x8 10.8 us: shards(): earlier.append(lax.ppermute(earlier[-1], 'inner', up))]
  transfers between devices with their start and end apart: 35 -> 49, of which waited for: 35 -> 46; matrix products, arithmetic and copies ran while one was open for 1% -> 1% of each run, Pallas kernels for 0% -> 0%
where the time goes in v1:
time: 977 us; the launch traced here: 970 us
  waiting for transfers between devices  404 us (41%)
  other arithmetic  188 us (19%)
  matrix products  155 us (16%)
  starting transfers between devices  109 us (11%)
  local copies, waits for them, and re-layouts  78.9 us (8%)
  loops' own time  17.5 us (2%)
  between operations  16.8 us (2%)
    ppermute x30, waiting for transfers between devices, from_behind(): return lax.ppermute(array, axis, pairs)  123 us
    reduce_scatter x1, waiting for transfers between devices, shards(): lax.psum_scatter((main_part + jnp.dot(grad_gates, gate_pair.T, preferred_...  91.8 us
    another operation x44, other arithmetic, block_step(): lax.linalg.triangular_solve(system, target, left_side=True, lower=True, u...  85.4 us
    reduce_scatter x1, waiting for transfers between devices, shards(): lax.psum_scatter(jnp.dot(scaled, down_weight, preferred_element_type=jnp....  75.8 us
    ppermute x30, starting transfers between devices, from_behind(): return lax.ppermute(array, axis, pairs)  68.4 us
    all_gather x1, waiting for transfers between devices, shards(): embedded = lax.all_gather(columns, 'inner', axis=1, tiled=True)  50.4 us
    all_gather x1, waiting for transfers between devices, shards(): lax.all_gather(grad_mixed, 'inner', axis=0, tiled=True)  47.3 us
    ppermute x7, starting transfers between devices, shards(): later.append(lax.ppermute(later[-1], 'inner', down))  39 us
  transfers between devices with their start and end apart: 49, of which 46 were waited for; matrix products, arithmetic and copies ran while one was open for 1% of the time, Pallas kernels for 0%

profile of v1, /device:TPU:32, one launch (start us, length us, event | category | flops | bytes accessed | tf_op | source)
XLA Modules:
  0.0 969.6 jit_solution(4271126712157413170)
XLA Ops:
  12.9 50.4 %all-gather.3.cloned.1.call-done = bf16[256,2048]{1,0:T(8,128)(2,1)} async-done(((bf16[256,128]{1,0:T(8,128)(2,1)}), bf16[256,2048]{1,0:T(8,128)(2,1)}) %all-gather.3.cloned.1.call-update) | async-done | bytes 1048592 | tf_op jit(solution)/shard_map/all_gather | solution.py:108
  72.2 75.8 %reduce-scatter.3.cloned.1.call-done = bf16[16,2048]{1,0:T(8,128)(2,1)} async-done(((bf16[256,2048]{1,0:T(8,128)(2,1)}), bf16[16,2048]{1,0:T(8,128)(2,1)}) %reduce-scatter.3.cloned.1.call-update) | async-done | bytes 65552 | tf_op jit(solution)/shard_map/reduce_scatter | solution.py:127
  151.5 6.4 collective-permute-done.2
  159.0 5.4 collective-permute-start.10
  166.7 5.4 collective-permute-start.11
  174.0 5.7 collective-permute-start.12
  183.2 5.4 collective-permute-start.13
  190.5 5.7 collective-permute-start.14
  198.1 5.7 collective-permute-start.15
  205.7 5.7 collective-permute-start.16
  222.5 42.1 %while.149 = (s32[]{:T(128)}, f32[1,128,384]{2,1,0:T(8,128)S(1)}, f32[4,1,64]{2,1,0:T(1,128)}, f32[4,1,64,128]{3,2,1,0:T(8,128)S(1)}, f32[4,1,64]{2,1,0:T(1,128)...) while((s32[]{:T(128)}, f32[1,128,384]{2,1,0:T(8,128)S(1)}, f32[4,1,64]{2,1,0:T(1,128)}, ...), condition=%wide.region_6.7_spmd, body=%wide.region_4.6_spmd.sunk | while | flops 100913216 | bytes 1219713 | solution.py:70
  266.7 111.0 %while.150 = (s32[]{:T(128)}, f32[1,128,256]{2,1,0:T(8,128)}, bf16[1,128,256]{2,1,0:T(8,128)(2,1)}, f32[1,128,128]{2,1,0:T(8,128)S(1)}, f32[1,128,256]{2,1,0:T(8,128)S(1)}, /*index=5*/s32[]{:T(128)}) while((s32[]{:T(128)}, f32[1,128,256]{2,1,0:T(8,128)}, bf16[1,128,256]{2,1,0:T(8,128)(2,1)}, f32[1,128,128]{2,1,0:T(8,128)S(1)}, ...), condition=%wide.region_8.9_spmd, body=%wide.region_7.8_spmd.sunk | while | flops 50429952 | bytes 786541 | solution.py:191
  361.2 5.5 collective-permute-start
  369.2 5.9 collective-permute-start
  380.5 95.2 %while.152 = (s32[]{:T(128)}, f32[1,128,256]{2,1,0:T(8,128)}, f32[4,1,64,64]{3,2,1,0:T(8,128)}, f32[4,1,128,64]{3,2,1,0:T(8,128)}, f32[4,1,64,64]{3,2,1,0:T(8,12...) while((s32[]{:T(128)}, f32[1,128,256]{2,1,0:T(8,128)}, ...), condition=%wide.region_12.13_spmd.clone.clone, body=%wide.region_10.12_spmd.clone.clone.sunk | while | flops 100962496 | bytes 2558033 | solution.py:70
  477.7 109.5 %while.154 = (s32[]{:T(128)}, f32[1,128,256]{1,2,0:T(8,128)S(1)}, f32[4,1,64,128]{3,2,1,0:T(8,128)}, f32[4,1,64,128]{3,2,1,0:T(8,128)}, f32[4,1,64,256]{3,2,1,0:...) while((s32[]{:T(128)}, f32[1,128,256]{1,2,0:T(8,128)S(1)}, ...), condition=%wide.region_24.27_spmd.clone.clone, body=%wide.region_13.26_spmd.clone.clone.sunk | while | flops 230404480 | bytes 3990816 | solution.py:70
  481.4 4.9 custom-call.53
  588.0 116.2 %while.151 = (s32[]{:T(128)}, f32[1,128,256]{2,1,0:T(8,128)}, bf16[1,128,256]{2,1,0:T(8,128)(2,1)S(1)}, f32[1,128,128]{2,1,0:T(8,128)S(1)}, f32[1,128,256]{2,1,0:T(8,128)S(1)}, /*index=5*/s32[]{:T(128)}) while((s32[]{:T(128)}, f32[1,128,256]{2,1,0:T(8,128)}, bf16[1,128,256]{2,1,0:T(8,128)(2,1)S(1)}, f32[1,128,128]{2,1,0:T(8,128)S(1)}, ...), condition=%wide.region_27.30_spmd, body=%wide.region_26.29_spmd.sunk | while | flops 50429952 | bytes 786541 | solution.py:242
  597.4 5.4 collective-permute-done.1
  613.1 5.4 collective-permute-done.1
  628.9 5.4 collective-permute-done.1
  707.3 103.9 %while.153 = (s32[]{:T(128)}, f32[1,128,256]{1,2,0:T(8,128)S(1)}, f32[4,1,64,128]{3,2,1,0:T(8,128)}, f32[4,1,64,128]{3,2,1,0:T(8,128)}, f32[4,1,64,256]{3,2,1,0:...) while((s32[]{:T(128)}, f32[1,128,256]{1,2,0:T(8,128)S(1)}, ...), condition=%wide.region_39.42_spmd.clone.clone, body=%wide.region_28.41_spmd.clone.clone.sunk | while | flops 230273408 | bytes 4006157 | solution.py:70
  818.7 91.8 %reduce-scatter.5.cloned.1.call-done = bf16[16,2048]{1,0:T(8,128)(2,1)} async-done(((bf16[256,2048]{1,0:T(8,128)(2,1)}), bf16[16,2048]{1,0:T(8,128)(2,1)}) %reduce-scatter.5.cloned.1.call-update) | async-done | bytes 65552 | tf_op jit(solution)/shard_map/reduce_scatter | solution.py:258
  913.3 47.3 %all-gather.5.cloned.1.call-done = bf16[256,2048]{1,0:T(8,128)(2,1)} async-done(((bf16[16,2048]{1,0:T(8,128)(2,1)}), bf16[256,2048]{1,0:T(8,128)(2,1)}) %all-gather.5.cloned.1.call-update) | async-done | bytes 1048592 | tf_op jit(solution)/shard_map/all_gather | solution.py:268
  (737 shorter events, 592.3 us)
Async XLA Ops:
  6.5 56.8 %all-gather.3.cloned.1.call-start = ((), (), s32[]{:S(2)}) async-start(), calls=%async_computation.2 | async-start | bytes 1114112 | tf_op jit(solution)/shard_map/all_gather | solution.py:108
  12.2 135.8 %reduce-scatter.3.cloned.1.call-start = ((), (), s32[]{:S(2)}) async-start(), calls=%async_computation.3 | async-start | bytes 1114112 | tf_op jit(solution)/shard_map/reduce_scatter | solution.py:127
  70.6 839.9 %reduce-scatter.5.cloned.1.call-start = ((), (), s32[]{:S(2)}) async-start(), calls=%async_computation.4 | async-start | bytes 1114112 | tf_op jit(solution)/shard_map/reduce_scatter | solution.py:258
  150.2 7.7 collective-permute-start.2
  157.9 7.6 collective-permute-start.3
  159.0 7.6 collective-permute-start.10
  165.5 7.6 collective-permute-start.4
  166.7 7.3 collective-permute-start.11
  173.1 7.8 collective-permute-start.5
  174.0 9.2 collective-permute-start.12
  180.9 8.0 collective-permute-start.6
  183.2 7.3 collective-permute-start.13
  188.9 7.6 collective-permute-start.7
  190.5 7.6 collective-permute-start.14
  196.5 7.6 collective-permute-start.8
  198.1 7.6 collective-permute-start.15
  204.0 7.6 collective-permute-start.9
  205.7 7.8 collective-permute-start.16
  369.2 7.0 collective-permute-start
  595.5 7.3 collective-permute-start.1
  611.2 7.3 collective-permute-start.1
  626.9 7.3 collective-permute-start.1
  658.1 6.8 collective-permute-start.1
  818.6 141.9 %all-gather.5.cloned.1.call-start = ((), (), s32[]{:S(2)}) async-start(), calls=%async_computation.5 | async-start | bytes 1114112 | tf_op jit(solution)/shard_map/all_gather | solution.py:268
  (71 other events, 2274.4 us)
Sparse Core Ops, SparseCore 0:
  12.4 50.9 all-gather.2
  70.7 77.3 reduce-scatter.2
  818.8 91.6 reduce-scatter.4
  913.4 47.1 all-gather.4
